TPU v7x, 512 devices: a whole 4x8x8 slice. The times are simulated.
512 devices in a mesh: section: 4 (over x_hi, core), feat: 128 (over y, z, x_lo).
Axes of the slice: x: 4 (x_hi: 2, x_lo: 2; x = x_hi * 2 + x_lo), y: 8, z: 8, core: 2. Of those that a mesh axis runs over, the one named last changes fastest.
Arguments:
- inputs: bfloat16 [4, 128, 8192], P('section', None, 'feat'), may hold values from -6 to 6
- targets: bfloat16 [4, 128, 8192], P('section', None, 'feat'), may hold values from -6 to 6
- enc_w: bfloat16 [4, 4096, 8192], P('section', 'feat'), may hold values from -0.0625 to 0.0625
- enc_b: float32 [4, 4096], P('section', 'feat'), may hold values from -3 to 3
- dec_w: bfloat16 [4, 2, 8192, 4096], P('section', None, 'feat'), may hold values from -0.375 to 0.375
- dec_b: float32 [4, 8192], P('section', 'feat'), may hold values from -3 to 3
Outputs:
- enc_grad: bfloat16 [4, 4096, 8192], P('section', 'feat')
- dec_grad: bfloat16 [4, 2, 8192, 4096], P('section', None, 'feat')
All inputs are finite; a program needn't handle non-finite values.
Results may differ from a plain program's by a relative error of at most 0.0058.
Values may be sent and summed in bfloat16 or wider, within the bound.
A program may use at most 64 MiB of HBM per device.

v0:
```python
import jax
import jax.numpy as jnp
from jax import lax
from jax.sharding import PartitionSpec as P


def from_behind(value, axis, steps):
    count = lax.axis_size(axis)
    initial, last = (max(0, -steps), min(count, count - steps))
    return lax.ppermute(value, axis, [(source, source + steps) for source in range(initial, last)])


def transposed(left, right):
    return lax.dot_general(
        left, right, (((0,), (0,)), ((), ())), preferred_element_type=jnp.float32
    )


def against(left, right):
    return lax.dot_general(
        left, right, (((1,), (1,)), ((), ())), preferred_element_type=jnp.float32
    )


def on_device(inputs, targets, enc_w, enc_b, dec_w, dec_b):
    scale = inputs.shape[1] ** (-0.5)
    reach = dec_w.shape[1]
    gathered = lax.all_gather(inputs[0], "feat", axis=1, tiled=True)
    pre = against(gathered, enc_w[0]) + enc_b[0]
    active = jnp.maximum(pre, 0.0)
    codes = (active * active).astype(jnp.bfloat16)
    own_codes = lax.all_gather(codes, "feat", axis=1, tiled=True)
    target = targets[0].astype(jnp.float32)
    weights = dec_w[0]
    code_grad = None
    sources = [own_codes]
    previous = own_codes
    previous = from_behind(previous, "section", 1)
    sources.append(previous)
    total = dec_b[0] + against(sources[0], weights[0])
    offset = 1
    total = total + against(sources[offset], weights[offset])
    error = ((total - target) * scale).astype(jnp.bfloat16)
    slots = [transposed(error, sources[offset]).astype(jnp.bfloat16) for offset in range(reach)]
    code_grad = jnp.dot(error, weights[0], preferred_element_type=jnp.float32)
    held_error = error
    held_weights = weights[1:]
    held_error, held_weights = from_behind((held_error, held_weights), "section", -1)
    code_grad = code_grad + jnp.dot(held_error, held_weights[0], preferred_element_type=jnp.float32)
    mine = lax.psum_scatter(code_grad, "feat", scatter_dimension=1, tiled=True)
    pre_grad = (mine * 2.0 * active).astype(jnp.bfloat16)
    enc_grad = transposed(pre_grad, gathered).astype(jnp.bfloat16)[None]
    dec_grad = jnp.stack(slots)[None]
    return (enc_grad, dec_grad)


def solution(mesh):
    return jax.shard_map(
        on_device,
        mesh=mesh,
        in_specs=(
            P("section", None, "feat"),
            P("section", None, "feat"),
            P("section", "feat", None),
            P("section", "feat"),
            P("section", None, "feat", None),
            P("section", "feat"),
        ),
        out_specs=(P("section", "feat", None), P("section", None, "feat", None)),
        check_vma=False,
    )
```

profile of v0, /device:TPU:4, one launch (start us, length us, event | category | flops | bytes accessed | tf_op | source)
XLA Modules:
  0.0 1848.6 jit_solution(361580426507441476)
XLA Ops:
  7.2 0.0 copy-start
  7.2 0.0 copy-start.2
  7.2 0.0 copy-start.4
  7.2 0.0 all-gather.6.cloned.1.call-start
  7.2 0.7 all-gather.6.cloned.1.call-update
  7.9 0.0 all-gather.4.cloned.1.call-start
  8.0 596.3 %all-gather.6.cloned.1.call-done = bf16[1,128,8192]{1,2,0:T(8,128)(2,1)} async-done(((bf16[1,128,64]{1,2,0:T(8,128)(2,1)}), bf16[1,128,8192]{1,2,0:T(8,128)(2,1)}) %all-gather.6.cloned.1.call-update) | async-done | bytes 2097168 | tf_op jit(solution)/shard_map/all_gather | solution.py:28
  604.3 0.0 copy-done
  604.3 2.7 multiply_convert_fusion.1
  607.0 0.0 all-gather.4.cloned.1.call-update
  607.0 0.0 reduce-scatter.2.cloned.1.call-start
  607.0 582.7 %all-gather.4.cloned.1.call-done = bf16[128,4096]{0,1:T(8,128)(2,1)} async-done(((bf16[128,32]{0,1:T(8,128)(2,1)}), bf16[128,4096]{0,1:T(8,128)(2,1)}) %all-gather.4.cloned.1.call-update) | async-done | bytes 1048592 | tf_op jit(solution)/shard_map/all_gather | solution.py:32
  1189.7 1.9 collective-permute-start
  1191.7 0.0 copy-done.2
  1191.7 5.1 collective-permute-start.2
  1196.9 0.0 copy-done.4
  1196.9 1.5 convolution_add_fusion.2
  1198.4 9.1 collective-permute-done
  1207.6 0.0 copy-done.3
  1207.6 0.3 fusion.8
  1207.9 1.9 collective-permute-start.1
  1209.8 0.5 fusion.17
  1210.4 0.0 collective-permute-done.2
  1210.4 0.9 collective-permute-done.1
  1211.2 1.8 convolution_add_fusion
  1213.1 0.0 reduce-scatter.2.cloned.1.call-update
  1213.1 0.5 fusion.2
  1213.6 0.0 copy-start.1
  1213.6 1.9 fusion.1
  1215.5 1.1 maximum_bitcast_fusion
  1216.5 623.2 %reduce-scatter.2.cloned.1.call-done = f32[128,32]{0,1:T(8,128)} async-done(((f32[128,4096]{0,1:T(8,128)}), f32[128,32]{0,1:T(8,128)}) %reduce-scatter.2.cloned.1.call-update) | async-done | bytes 16400 | tf_op jit(solution)/shard_map/reduce_scatter | solution.py:50
  1839.7 2.3 fusion
  (3 shorter events, 0.0 us)
Async XLA Ops:
  7.2 597.1 %copy-start = (bf16[1,32,8192]{2,1,0:T(8,128)(2,1)S(1)}, bf16[1,32,8192]{2,1,0:T(8,128)(2,1)}, u32[]{:S(2)}) copy-start(bf16[1,32,8192]{2,1,0:T(8,128)(2,1)} %param.8) | copy-start | bytes 1572868
  7.2 1184.5 %copy-start.2 = (bf16[1,2,64,4096]{3,2,1,0:T(8,128)(2,1)S(1)}, bf16[1,2,64,4096]{3,2,1,0:T(8,128)(2,1)}, u32[]{:S(2)}) copy-start(bf16[1,2,64,4096]{3,2,1,0:T(8,128)(2,1)} %param.10) | copy-start | bytes 3145732
  7.2 1189.7 %copy-start.4 = (f32[1,64]{1,0:T(1,128)S(1)}, f32[1,64]{1,0:T(1,128)}, u32[]{:S(2)}) copy-start(f32[1,64]{1,0:T(1,128)} %param.11) | copy-start | bytes 772
  7.2 597.1 %all-gather.6.cloned.1.call-start = ((), (), s32[]{:S(2)}) async-start(), calls=%async_computation.3 | async-start | bytes 2113536 | tf_op jit(solution)/shard_map/all_gather | solution.py:28
  7.9 1181.8 %all-gather.4.cloned.1.call-start = ((), (), s32[]{:S(2)}) async-start(), calls=%async_computation.1 | async-start | bytes 1056768 | tf_op jit(solution)/shard_map/all_gather | solution.py:32
  604.3 603.3 %copy-start.3 = (bf16[1,128,64]{1,2,0:T(8,128)(2,1)S(1)}, bf16[1,128,64]{1,2,0:T(8,128)(2,1)}, u32[]{:S(2)}) copy-start(bf16[1,128,64]{1,2,0:T(8,128)(2,1)} %param.7) | copy-start | bytes 49156
  607.0 1232.7 %reduce-scatter.2.cloned.1.call-start = ((), (), s32[]{:S(2)}) async-start(), calls=%async_computation.2 | async-start | bytes 2113536 | tf_op jit(solution)/shard_map/reduce_scatter | solution.py:50
  1189.7 17.8 collective-permute-start
  1191.7 18.6 %collective-permute-start.2 = (bf16[1,64,4096]{2,1,0:T(8,128)(2,1)S(1)}, bf16[1,64,4096]{2,1,0:T(8,128)(2,1)S(1)}, u32[]{:S(2)}, u32[]{:S(2)}) collective-permute-start(bf16[1,64,4096]{2,1,0:T(8,128)(2,1)S(1)} %slice_bitcast_fusion), channel_id=1, source_target_pairs={{128,0},{256,128},{384,256},{129,1},{257,129},{385,257},{130,2},{2... | collective-permute-start | bytes 1572872 | tf_op jit(solution)/shard_map/ppermute | solution.py:10
  1207.9 3.4 collective-permute-start.1
  1213.6 626.2 %copy-start.1 = (bf16[1,128,8192]{1,2,0:T(8,128)(2,1)S(1)}, bf16[1,128,8192]{1,2,0:T(8,128)(2,1)}, u32[]{:S(2)}) copy-start(bf16[1,128,8192]{1,2,0:T(8,128)(2,1)} %all-gather.6.cloned.1.call-done) | copy-start | bytes 6291460
Sparse Core Ops, SparseCore 0:
  10.1 594.1 all-gather.5
  607.1 582.5 all-gather.3
  1213.2 626.4 reduce-scatter.1
where the time goes:
time: 1850 us
  waiting for transfers between devices  1810 us (98%)
    reduce_scatter x1, waiting for transfers between devices, on_device(): mine = lax.psum_scatter(code_grad, 'feat', scatter_dimension=1, tiled=True)  623 us
    all_gather x1, waiting for transfers between devices, on_device(): gathered = lax.all_gather(inputs[0], 'feat', axis=1, tiled=True)  596 us
    all_gather x1, waiting for transfers between devices, on_device(): own_codes = lax.all_gather(codes, 'feat', axis=1, tiled=True)  583 us
  transfers between devices with their start and end apart: 6, of which 5 were waited for; matrix products, arithmetic and copies ran while one was open for 0% of the time, Pallas kernels for 0%

commit v1 on v0

--- a/solution.py
+++ b/solution.py
@@ -25,7 +25,9 @@
 def on_device(inputs, targets, enc_w, enc_b, dec_w, dec_b):
     scale = inputs.shape[1] ** (-0.5)
     reach = dec_w.shape[1]
-    gathered = lax.all_gather(inputs[0], "feat", axis=1, tiled=True)
+    gathered = jnp.concatenate(
+        lax.all_to_all(jnp.stack([inputs[0]] * lax.axis_size("feat")), "feat", 0, 0), axis=1
+    )
     pre = against(gathered, enc_w[0]) + enc_b[0]
     active = jnp.maximum(pre, 0.0)
     codes = (active * active).astype(jnp.bfloat16)

time: 1850 us -> 1320 us (0.71)
  waiting for transfers between devices: 1810 us -> 1220 us
  blocking collectives: 0 us -> 70.2 us
    all_gather x1 -> x0, waiting for transfers between devices: 596 us -> none  [on_device(): gathered = lax.all_gather(inputs[0], 'feat', axis=1, tiled=True)]
    all_to_all x0 -> x1, blocking collectives: none -> 70.2 us  [on_device(): lax.all_to_all(jnp.stack([inputs[0]] * lax.axis_size('feat')), 'feat', 0, 0)]
  transfers between devices with their start and end apart: 6 -> 5, of which waited for: 5 -> 4; matrix products, arithmetic and copies ran while one was open for 0% -> 1% of each run, Pallas kernels for 0% -> 0%
where the time goes in v1:
time: 1320 us
  waiting for transfers between devices  1220 us (92%)
  blocking collectives  70.2 us (5%)
  between operations  14.2 us (1%)
    reduce_scatter x1, waiting for transfers between devices, on_device(): mine = lax.psum_scatter(code_grad, 'feat', scatter_dimension=1, tiled=True)  623 us
    all_gather x1, waiting for transfers between devices, on_device(): own_codes = lax.all_gather(codes, 'feat', axis=1, tiled=True)  583 us
    all_to_all x1, blocking collectives, on_device(): lax.all_to_all(jnp.stack([inputs[0]] * lax.axis_size('feat')), 'feat', 0, 0)  70.2 us
  transfers between devices with their start and end apart: 5, of which 4 were waited for; matrix products, arithmetic and copies ran while one was open for 1% of the time, Pallas kernels for 0%

profile of v1, /device:TPU:4, one launch (start us, length us, event | category | flops | bytes accessed | tf_op | source)
XLA Modules:
  0.0 1323.2 jit_solution(15397324210150074424)
XLA Ops:
  7.2 0.0 copy-start
  7.2 0.0 all-gather.2.cloned.1.call-start
  7.2 1.3 stack.12
  8.5 0.0 copy-start.6
  8.5 70.2 %all_to_all.5 = bf16[128,128,64]{1,2,0:T(8,128)(2,1)S(1)} all-to-all(bf16[128,128,64]{1,2,0:T(8,128)(2,1)S(1)} %stack.12), channel_id=1, replica_groups=mesh['section'=4,'feat'=128] {'feat'}, dimensions={0} | all-to-all | bytes 4194304 | tf_op jit(solution)/shard_map/all_to_all | solution.py:29
  78.7 0.0 copy-done
  78.7 0.0 copy-done.6
  78.8 1.1 multiply_convert_fusion.1
  79.8 0.0 all-gather.2.cloned.1.call-update
  79.8 0.0 reduce-scatter.2.cloned.1.call-start
  79.9 583.3 %all-gather.2.cloned.1.call-done = bf16[128,4096]{0,1:T(8,128)(2,1)} async-done(((bf16[128,32]{0,1:T(8,128)(2,1)}), bf16[128,4096]{0,1:T(8,128)(2,1)}) %all-gather.2.cloned.1.call-update) | async-done | bytes 1048592 | tf_op jit(solution)/shard_map/all_gather | solution.py:34
  663.2 2.0 collective-permute-start
  665.2 1.1 slice_bitcast_fusion
  666.3 5.1 collective-permute-start.2
  671.5 0.0 copy-done.5
  671.5 1.7 convolution_add_fusion.2
  673.2 7.9 collective-permute-done
  681.1 0.0 copy-done.4
  681.1 0.0 copy-done.1
  681.2 0.3 fusion.5
  681.5 0.6 copy-done.3
  682.1 1.9 collective-permute-start.1
  684.0 0.5 fusion.9
  684.6 0.0 collective-permute-done.2
  684.6 0.9 collective-permute-done.1
  685.5 1.9 convolution_add_fusion
  687.3 0.0 reduce-scatter.2.cloned.1.call-update
  687.4 1.8 fusion.2
  689.2 0.5 fusion.1
  689.7 1.1 maximum_bitcast_fusion
  690.7 623.3 %reduce-scatter.2.cloned.1.call-done = f32[128,32]{0,1:T(8,128)} async-done(((f32[128,4096]{0,1:T(8,128)}), f32[128,32]{0,1:T(8,128)}) %reduce-scatter.2.cloned.1.call-update) | async-done | bytes 16400 | tf_op jit(solution)/shard_map/reduce_scatter | solution.py:52
  1314.0 2.3 fusion
  (6 shorter events, 0.0 us)
Async XLA Ops:
  7.2 71.6 %copy-start = (bf16[1,32,8192]{2,1,0:T(8,128)(2,1)S(1)}, bf16[1,32,8192]{2,1,0:T(8,128)(2,1)}, u32[]{:S(2)}) copy-start(bf16[1,32,8192]{2,1,0:T(8,128)(2,1)} %param.8) | copy-start | bytes 1572868
  7.2 656.0 %all-gather.2.cloned.1.call-start = ((), (), s32[]{:S(2)}) async-start(), calls=%async_computation.2 | async-start | bytes 1056768 | tf_op jit(solution)/shard_map/all_gather | solution.py:34
  8.5 70.2 %copy-start.6 = (f32[1,32]{1,0:T(1,128)S(1)}, f32[1,32]{1,0:T(1,128)}, u32[]{:S(2)}) copy-start(f32[1,32]{1,0:T(1,128)} %param.9) | copy-start | bytes 388
  78.7 592.7 %copy-start.5 = (f32[1,64]{1,0:T(1,128)S(1)}, f32[1,64]{1,0:T(1,128)}, u32[]{:S(2)}) copy-start(f32[1,64]{1,0:T(1,128)} %param.11) | copy-start | bytes 772
  78.7 602.4 %copy-start.4 = (bf16[1,128,64]{1,2,0:T(8,128)(2,1)S(1)}, bf16[1,128,64]{1,2,0:T(8,128)(2,1)}, u32[]{:S(2)}) copy-start(bf16[1,128,64]{1,2,0:T(8,128)(2,1)} %param.7) | copy-start | bytes 49156
  79.8 1234.2 %reduce-scatter.2.cloned.1.call-start = ((), (), s32[]{:S(2)}) async-start(), calls=%async_computation.3 | async-start | bytes 2113536 | tf_op jit(solution)/shard_map/reduce_scatter | solution.py:52
  663.2 18.0 %copy-start.1 = (bf16[1,2,64,4096]{3,2,1,0:T(8,128)(2,1)S(1)}, bf16[1,2,64,4096]{3,2,1,0:T(8,128)(2,1)}, u32[]{:S(2)}) copy-start(bf16[1,2,64,4096]{3,2,1,0:T(8,128)(2,1)} %param.10) | copy-start | bytes 3145732
  663.2 18.0 %collective-permute-start = (bf16[128,4096]{0,1:T(8,128)(2,1)}, bf16[128,4096]{0,1:T(8,128)(2,1)S(1)}, u32[]{:S(2)}, u32[]{:S(2)}) collective-permute-start(bf16[128,4096]{0,1:T(8,128)(2,1)} %all-gather.2.cloned.1.call-done), channel_id=1, source_target_pairs={{0,128},{128,256},{256,384},{1,129},{129,257},{257,385},{2,130},{1... | collective-permute-start | bytes 3145736 | tf_op jit(solution)/shard_map/ppermute | solution.py:10
  666.3 18.3 %collective-permute-start.2 = (bf16[1,64,4096]{2,1,0:T(8,128)(2,1)S(1)}, bf16[1,64,4096]{2,1,0:T(8,128)(2,1)S(1)}, u32[]{:S(2)}, u32[]{:S(2)}) collective-permute-start(bf16[1,64,4096]{2,1,0:T(8,128)(2,1)S(1)} %slice_bitcast_fusion), channel_id=1, source_target_pairs={{128,0},{256,128},{384,256},{129,1},{257,129},{385,257},{130,2},{2... | collective-permute-start | bytes 1572872 | tf_op jit(solution)/shard_map/ppermute | solution.py:10
  681.1 1.0 copy-start.3
  682.1 3.3 collective-permute-start.1
  687.4 1.8 copy-start.2
Sparse Core Ops, SparseCore 0:
  80.0 583.1 all-gather.1
  687.5 626.4 reduce-scatter.1
